TPU v7x, 32 devices: a whole 2x2x4 slice. The times are simulated.
32 devices in a mesh: space: 16 (over z, y, core), filt: 2 (over x).
Axes of the slice: x: 2, y: 2, z: 4, core: 2. Of those that a mesh axis runs over, the one named last changes fastest.
Arguments:
- volume: bfloat16 [64, 32, 4, 256], P(None, 'space', 'filt'), may hold values from -6 to 6
- first_weight: bfloat16 [27, 64, 64], replicated, may hold values from -0.15625 to 0.15625
- second_weight: bfloat16 [27, 128, 64], P(None, 'filt'), may hold values from -0.15625 to 0.15625
- cotangent: bfloat16 [128, 16, 2, 128], P('filt', 'space'), may hold values from -24 to 24
Outputs:
- features: bfloat16 [128, 16, 2, 128], P('filt', 'space')
- volume_grad: bfloat16 [64, 32, 4, 256], P(None, 'space', 'filt')
- first_grad: float32 [27, 64, 64], replicated
- second_grad: float32 [27, 128, 64], P(None, 'filt')
All inputs are finite; a program needn't handle non-finite values.
Results may differ from a plain program's by a relative error of at most 0.019.
Values may be sent and summed in bfloat16 or wider, within the bound.
No kernel may reach another device: no remote copies, remote signals or barrier semaphores. Data moves between devices by JAX's collectives and lax.ppermute only.
A program may use at most 64 MiB of HBM per device.

v0:
```python
import jax
import jax.numpy as jnp
from jax import lax
from jax.sharding import PartitionSpec as P


def extended(cells, sides, width):
    for axis, dim in sides:
        count = lax.axis_size(axis)
        ends = count - 1
        head = lax.slice_in_dim(cells, 0, width, axis=dim)
        tail = lax.slice_in_dim(cells, cells.shape[dim] - width, cells.shape[dim], axis=dim)
        cells = jnp.concatenate(
            [
                lax.ppermute(tail, axis, [(i, (i + 1) % count) for i in range(ends)]),
                cells,
                lax.ppermute(head, axis, [((i + 1) % count, i) for i in range(ends)]),
            ],
            axis=dim,
        )
    return cells


def silu_slope(values):
    sigmoid_part = jax.nn.sigmoid(values)
    return sigmoid_part * (1.0 + values * (1.0 - sigmoid_part))


def pad_depth(volume_field):
    return jnp.pad(volume_field, ((0, 0), (0, 0), (0, 0), (1, 1)))


def window(padded, offset_x, offset_y, offset_z, extents):
    extent_x, extent_y, extent_z = extents
    section = lax.slice(
        padded,
        (0, offset_x, offset_y, offset_z),
        (padded.shape[0], offset_x + extent_x, offset_y + extent_y, offset_z + extent_z),
    )
    return section.reshape(padded.shape[0], extent_x * extent_y * extent_z)


def conv_forward(padded, weight, extents):
    outputs, inputs = (weight.shape[1], weight.shape[2])
    running = jnp.zeros((outputs, extents[0] * extents[1] * extents[2]), jnp.float32)
    for offset_x in range(3):
        for offset_y in range(3):
            tap_base = offset_x * 9 + offset_y * 3
            stacked = jnp.concatenate(
                [window(padded, offset_x, offset_y, offset_z, extents) for offset_z in range(3)],
                axis=0,
            )
            matrices = jnp.transpose(weight[tap_base : tap_base + 3], (1, 0, 2)).reshape(
                outputs, 3 * inputs
            )
            running = running + jnp.dot(matrices, stacked, preferred_element_type=jnp.float32)
    return running


def conv_transpose(padded, weight, extents):
    outputs, inputs = (weight.shape[1], weight.shape[2])
    running = jnp.zeros((inputs, extents[0] * extents[1] * extents[2]), jnp.float32)
    for offset_x in range(3):
        for offset_y in range(3):
            tap_base = offset_x * 9 + offset_y * 3
            stacked = jnp.concatenate(
                [window(padded, offset_x, offset_y, offset_z, extents) for offset_z in range(3)],
                axis=0,
            )
            tap_block = weight[24 - tap_base : 27 - tap_base][::-1]
            matrices = jnp.transpose(tap_block, (2, 0, 1)).reshape(inputs, 3 * outputs)
            running = running + jnp.dot(matrices, stacked, preferred_element_type=jnp.float32)
    return running


def conv_weights(grad_rows, padded, extents):
    outputs, inputs = (grad_rows.shape[0], padded.shape[0])
    blocks = []
    for offset_x in range(3):
        for offset_y in range(3):
            stacked = jnp.concatenate(
                [window(padded, offset_x, offset_y, offset_z, extents) for offset_z in range(3)],
                axis=0,
            )
            section = lax.dot_general(
                grad_rows, stacked, (((1,), (1,)), ((), ())), preferred_element_type=jnp.float32
            )
            blocks.append(jnp.transpose(section.reshape(outputs, 3, inputs), (1, 0, 2)))
    return jnp.concatenate(blocks, axis=0)


def pool_cells(hidden):
    channels, size_x, size_y, size_z = hidden.shape
    pair_table = (jnp.arange(size_z)[:, None] // 2 == jnp.arange(size_z // 2)[None, :]).astype(
        jnp.bfloat16
    )
    depth_sums = jnp.dot(hidden.reshape(-1, size_z), pair_table, preferred_element_type=jnp.float32)
    depth_sums = depth_sums.reshape(channels, size_x // 2, 2, size_y // 2, 2, size_z // 2)
    return (0.125 * depth_sums.sum(axis=(2, 4))).astype(jnp.bfloat16)


def spread_cells(grad_field):
    scaled = 0.125 * grad_field
    scaled = jnp.repeat(scaled, 2, axis=1)
    scaled = jnp.repeat(scaled, 2, axis=2)
    return jnp.repeat(scaled, 2, axis=3)


def local(volume, first_weight, second_weight, cotangent):
    count_space = lax.axis_size("space")
    count_filt = lax.axis_size("filt")
    channels = volume.shape[0]
    fine_shape = volume.shape[1:]
    fine_cells = fine_shape[0] * fine_shape[1] * fine_shape[2] * count_space * count_filt
    fine_scale = 1.0 / fine_cells**0.5
    padded_in = pad_depth(extended(volume, (("space", 1), ("filt", 2)), 1))
    first_pre = conv_forward(padded_in, first_weight, fine_shape)
    hidden = jax.nn.silu(first_pre).astype(jnp.bfloat16).reshape((channels,) + fine_shape)
    pooled = pool_cells(hidden)
    brick_shape = pooled.shape[1:]
    brick_cells = brick_shape[0] * brick_shape[1] * brick_shape[2]
    bottom_scale = 1.0 / (brick_cells * count_space * count_filt) ** 0.5
    filters = second_weight.shape[1]
    whole_weight = lax.all_gather(second_weight, "filt", axis=1, tiled=True)
    total_filters = whole_weight.shape[1]
    padded_pool = pad_depth(extended(pooled, (("space", 1), ("filt", 2)), 1))
    second_pre = conv_forward(padded_pool, whole_weight, brick_shape)
    local_out = jax.nn.silu(second_pre).astype(jnp.bfloat16).reshape((total_filters,) + brick_shape)
    features = lax.all_to_all(local_out, "filt", split_axis=0, concat_axis=2, tiled=True)
    local_cot = lax.all_to_all(cotangent, "filt", split_axis=2, concat_axis=0, tiled=True)
    down_grad = (
        local_cot.reshape(total_filters, -1).astype(jnp.float32) * silu_slope(second_pre)
    ).astype(jnp.bfloat16)
    summed = lax.psum(conv_weights(down_grad, padded_pool, brick_shape), ("space", "filt"))
    second_grad = (
        lax.dynamic_slice_in_dim(summed, lax.axis_index("filt") * filters, filters, 1)
        * bottom_scale
    )
    padded_down = pad_depth(
        extended(down_grad.reshape((total_filters,) + brick_shape), (("space", 1), ("filt", 2)), 1)
    )

    def add_group(group_index, running):
        group_rows = lax.dynamic_slice_in_dim(padded_down, group_index * filters, filters, 0)
        tap_block = lax.dynamic_slice_in_dim(whole_weight, group_index * filters, filters, 1)
        section = conv_transpose(group_rows, tap_block, brick_shape)
        return running + lax.optimization_barrier(section.astype(jnp.bfloat16)).astype(jnp.float32)

    pool_grad = lax.fori_loop(
        0, count_filt, add_group, jnp.zeros((channels, brick_cells), jnp.float32)
    )
    hidden_grad = spread_cells(pool_grad.reshape((channels,) + brick_shape))
    first_down = (hidden_grad.reshape(channels, -1) * silu_slope(first_pre)).astype(jnp.bfloat16)
    first_grad = (
        lax.psum(conv_weights(first_down, padded_in, fine_shape), ("space", "filt")) * fine_scale
    )
    padded_back = pad_depth(
        extended(first_down.reshape((channels,) + fine_shape), (("space", 1), ("filt", 2)), 1)
    )
    volume_grad = (
        conv_transpose(padded_back, first_weight, fine_shape)
        .astype(jnp.bfloat16)
        .reshape((channels,) + fine_shape)
    )
    return (features, volume_grad, first_grad, second_grad)


def solution(mesh):
    placed = (
        P(None, "space", "filt", None),
        P(),
        P(None, "filt", None),
        P("filt", "space", None, None),
    )
    return jax.shard_map(
        local,
        mesh=mesh,
        in_specs=placed,
        out_specs=(
            P("filt", "space", None, None),
            P(None, "space", "filt", None),
            P(),
            P(None, "filt", None),
        ),
        check_vma=False,
    )
```

profile of v0, /device:TPU:0, one launch (start us, length us, event | category | flops | bytes accessed | tf_op | source)
XLA Modules:
  0.0 316.7 jit_solution(11860188222224926915)
XLA Ops:
  7.2 1.4 copy.107
  8.5 4.2 %all-to-all-start.1 = ((bf16[64,1,2,128]{3,0,1,2:T(8,128)(2,1)}), bf16[64,1,2,128]{3,0,1,2:T(8,128)(2,1)}, u32[]{:S(2)}, u32[]{:S(2)}) async-start(bf16[64,1,2,128]{3,0,1,2:T(8,128)(2,1)} %copy.107), calls=%async_computation.1 | async-start | bytes 65536 | tf_op jit(solution)/shard_map/all_to_all | solution.py:130
  12.8 1.0 fusion.162
  13.7 1.3 collective-permute-start.1
  15.0 3.0 collective-permute-start
  18.1 1.3 copy.96
  19.4 15.2 %all_gather.3 = bf16[27,128,64]{2,0,1:T(8,128)(2,1)S(1)} all-gather(bf16[27,64,64]{2,0,1:T(8,128)(2,1)S(1)} %copy.96), channel_id=1, replica_groups=mesh['space'=16,'filt'=2] {'filt'}, dimensions={1}, use_global_device_ids=true | all-gather | bytes 663552 | tf_op jit(solution)/shard_map/all_gather | solution.py:124
  34.6 1.3 fusion.155
  36.4 1.2 fusion.160
  37.6 4.2 %collective-permute-start.2 = (bf16[64,4,1,256]{3,2,1,0:T(2,128)(2,1)}, bf16[64,4,1,256]{3,2,1,0:T(2,128)(2,1)S(1)}, u32[]{:S(2)}, u32[]{:S(2)}) collective-permute-start(bf16[64,4,1,256]{3,2,1,0:T(2,128)(2,1)} %get-tuple-element.266), channel_id=1, source_target_pairs={{0,1},{2,3},{4,5},{6,7},{8,9},{10,11},{12,13},{14,15},{16,17},{18,... | collective-permute-start | bytes 393224 | tf_op jit(solution)/shard_map/ppermute | solution.py:15
  41.8 1.5 collective-permute-start.3
  43.3 1.0 fusion.158
  45.5 1.8 copy.153
  47.3 1.0 copy.152
  48.3 1.6 copy.151
  50.0 1.6 copy.150
  51.6 1.6 copy.149
  56.1 1.4 rev.98
  70.2 1.7 pad_maximum_fusion.9
  75.6 2.4 select_maximum_fusion.2
  78.1 2.9 fusion.157
  86.4 1.0 constant_dynamic-update-slice_fusion.11
  87.3 0.9 constant_dynamic-update-slice_fusion.14
  91.8 0.9 multiply_convert_fusion.1
  93.1 1.3 collective-permute-start.5
  94.4 3.0 collective-permute-start.4
  97.5 0.8 bitcast_convert_fusion
  98.4 1.3 collective-permute-start.7
  99.7 4.8 %collective-permute-start.6 = (bf16[64,3,1,128]{3,0,2,1:T(8,128)(2,1)S(1)}, bf16[64,3,1,128]{3,0,2,1:T(8,128)(2,1)S(1)}, u32[]{:S(2)}, u32[]{:S(2)}) collective-permute-start(bf16[64,3,1,128]{3,0,2,1:T(8,128)(2,1)S(1)} %pad_maximum_fusion.18), channel_id=1, source_target_pairs={{0,1},{2,3},{4,5},{6,7},{8,9},{10,11},{12,13},{14,15},{16,17},{18,... | collective-permute-start | bytes 147464 | tf_op jit(solution)/shard_map/ppermute | solution.py:15
  104.5 1.5 collective-permute-done.6
  108.2 1.3 collective-permute-start.9
  109.5 3.3 %collective-permute-start.8 = (bf16[128,1,1,128]{0,3,2,1:T(8,128)(2,1)S(1)}, bf16[128,1,1,128]{0,3,2,1:T(8,128)(2,1)S(1)}, u32[]{:S(2)}, u32[]{:S(2)}) collective-permute-start(bf16[128,1,1,128]{0,3,2,1:T(8,128)(2,1)S(1)} %bitcast.409), channel_id=1, source_target_pairs={{0,2},{2,4},{4,6},{6,8},{8,10},{10,12},{12,14},{14,16},{16,18},{18... | collective-permute-start | bytes 98312 | tf_op jit(solution)/shard_map/ppermute | solution.py:15
  115.9 3.3 %all-to-all-start = ((bf16[2,2,4096]{2,1,0:T(2,128)(2,1)}), bf16[2,2,4096]{2,1,0:T(2,128)(2,1)S(1)}, u32[]{:S(2)}, u32[]{:S(2)}) async-start(bf16[2,2,4096]{2,1,0:T(2,128)(2,1)} %reshape.942), calls=%async_computation | async-start | bytes 65536 | tf_op jit(solution)/shard_map/all_to_all | solution.py:129
  119.6 0.8 copy.127
  120.4 0.8 copy.126
  121.2 0.8 copy.125
  122.1 0.8 copy.124
  122.9 0.8 copy.123
  123.7 0.9 bitcast_dynamic-update-slice_fusion.8
  124.6 0.9 bitcast_dynamic-update-slice_fusion.7
  125.6 0.9 bitcast_dynamic-update-slice_fusion.6
  126.5 0.9 bitcast_dynamic-update-slice_fusion.5
  127.5 0.9 bitcast_dynamic-update-slice_fusion.4
  128.8 1.3 collective-permute-start.11
  130.1 4.6 %collective-permute-start.10 = (bf16[128,3,1,128]{0,3,2,1:T(8,128)(2,1)S(1)}, bf16[128,3,1,128]{0,3,2,1:T(8,128)(2,1)S(1)}, u32[]{:S(2)}, u32[]{:S(2)}) collective-permute-start(bf16[128,3,1,128]{0,3,2,1:T(8,128)(2,1)S(1)} %pad_maximum_fusion.17), channel_id=1, source_target_pairs={{0,1},{2,3},{4,5},{6,7},{8,9},{10,11},{12,13},{14,15},{16,17},{18,... | collective-permute-start | bytes 294920 | tf_op jit(solution)/shard_map/ppermute | solution.py:15
  134.8 0.8 copy.132
  135.6 1.3 collective-permute-done.10
  137.4 5.5 %while.14 = (s32[]{:T(128)}, f32[64,128]{1,0:T(8,128)}, bf16[27,128,64]{2,1,0:T(8,128)(2,1)S(1)}, bf16[128,3,3,130]{3,0,2,1:T(8,128)(2,1)S(1)}, s32[]{:T(128)}, ...) while((s32[]{:T(128)}, f32[64,128]{1,0:T(8,128)}, ...), condition=%wide.region_2.3_spmd.clone, body=%wide.region_1.2_spmd.clone.sunk | while | flops 29736976 | bytes 3318213 | solution.py:149
  142.9 0.9 broadcast_multiply_fusion.1
  147.0 1.3 collective-permute-start.13
  148.3 4.5 %collective-permute-start.12 = (bf16[64,1,2,256]{3,2,1,0:T(2,128)(2,1)S(1)}, bf16[64,1,2,256]{3,2,1,0:T(2,128)(2,1)S(1)}, u32[]{:S(2)}, u32[]{:S(2)}) collective-permute-start(bf16[64,1,2,256]{3,2,1,0:T(2,128)(2,1)S(1)} %get-tuple-element.272), channel_id=1, source_target_pairs={{0,2},{2,4},{4,6},{6,8},{8,10},{10,12},{12,14},{14,16},{16,18},{18... | collective-permute-start | bytes 196616 | tf_op jit(solution)/shard_map/ppermute | solution.py:15
  154.6 4.0 %collective-permute-start.14 = (bf16[64,4,1,256]{3,2,1,0:T(2,128)(2,1)S(1)}, bf16[64,4,1,256]{3,2,1,0:T(2,128)(2,1)S(1)}, u32[]{:S(2)}, u32[]{:S(2)}) collective-permute-start(bf16[64,4,1,256]{3,2,1,0:T(2,128)(2,1)S(1)} %get-tuple-element.261), channel_id=1, source_target_pairs={{0,1},{2,3},{4,5},{6,7},{8,9},{10,11},{12,13},{14,15},{16,17},{18,... | collective-permute-start | bytes 393224 | tf_op jit(solution)/shard_map/ppermute | solution.py:15
  158.6 1.6 collective-permute-start.15
  160.2 0.9 copy-done.20
  161.3 2.3 collective-permute-done.14
  163.6 4.7 %collective-permute-done.15 = bf16[64,4,1,256]{3,2,1,0:T(2,128)(2,1)S(1)} collective-permute-done((bf16[64,4,1,256]{3,2,1,0:T(2,128)(2,1)S(1)}, bf16[64,4,1,256]{3,2,1,0:T(2,128)(2,1)S(1)}, u32[]{:S(2)}, u32[]{:S(2)}) %collective-permute-start.15) | collective-permute-done | bytes 131104 | tf_op jit(solution)/shard_map/ppermute | solution.py:17
  168.3 1.7 pad_maximum_fusion.1
  172.4 2.4 select_maximum_fusion
  174.8 2.9 fusion.156
  181.8 1.2 fusion.62
  186.0 120.2 %all-reduce.7.cloned.1.call-done = (f32[27,64,64]{1,2,0:T(8,128)}, f32[27,128,64]{2,1,0:T(8,128)}) async-done(((f32[27,64,64]{1,2,0:T(8,128)}, f32[27,128,64]{2,1,0:T(8,128)}), (f32[27,64,64]{1,2,0:T(8,128)}, f32[27,128,64]{2,1,0:T(8,128)})) %all-reduce.7.cloned.1.call-update) | async-done | bytes 1327120 | tf_op jit(solution)/shard_map/psum | solution.py:155
  306.2 1.4 broadcast_multiply_fusion
  307.6 1.2 copy.133
  308.9 1.0 dynamic-slice_multiply_fusion
  (443 shorter events, 55.2 us)
Async XLA Ops:
  8.5 88.9 %all-to-all-start.1 = ((bf16[64,1,2,128]{3,0,1,2:T(8,128)(2,1)}), bf16[64,1,2,128]{3,0,1,2:T(8,128)(2,1)}, u32[]{:S(2)}, u32[]{:S(2)}) async-start(bf16[64,1,2,128]{3,0,1,2:T(8,128)(2,1)} %copy.107), calls=%async_computation.1 | async-start | bytes 65536 | tf_op jit(solution)/shard_map/all_to_all | solution.py:130
  13.7 22.2 %collective-permute-start.1 = (bf16[64,1,2,256]{3,2,1,0:T(2,128)(2,1)S(1)}, bf16[64,1,2,256]{3,2,1,0:T(2,128)(2,1)S(1)}, u32[]{:S(2)}, u32[]{:S(2)}) collective-permute-start(bf16[64,1,2,256]{3,2,1,0:T(2,128)(2,1)S(1)} %get-tuple-element.276), channel_id=1, source_target_pairs={{2,0},{4,2},{6,4},{8,6},{10,8},{12,10},{14,12},{16,14},{18,16},{20... | collective-permute-start | bytes 196616 | tf_op jit(solution)/shard_map/ppermute | solution.py:17
  15.0 20.9 %collective-permute-start = (bf16[64,1,2,256]{3,2,1,0:T(2,128)(2,1)S(1)}, bf16[64,1,2,256]{3,2,1,0:T(2,128)(2,1)S(1)}, u32[]{:S(2)}, u32[]{:S(2)}) collective-permute-start(bf16[64,1,2,256]{3,2,1,0:T(2,128)(2,1)S(1)} %get-tuple-element.277), channel_id=1, source_target_pairs={{0,2},{2,4},{4,6},{6,8},{8,10},{10,12},{12,14},{14,16},{16,18},{18... | collective-permute-start | bytes 196616 | tf_op jit(solution)/shard_map/ppermute | solution.py:15
  19.4 16.6 %copy-start.17 = (bf16[64,2,2,256]{3,2,1,0:T(2,128)(2,1)S(1)}, bf16[64,2,2,256]{3,2,1,0:T(2,128)(2,1)}, u32[]{:S(2)}) copy-start(bf16[64,2,2,256]{3,2,1,0:T(2,128)(2,1)} %param.6) | copy-start | bytes 393220
  34.6 8.6 %copy-start.35 = (bf16[27,64,64]{2,1,0:T(8,128)(2,1)S(1)}, bf16[27,64,64]{2,1,0:T(8,128)(2,1)}, u32[]{:S(2)}) copy-start(bf16[27,64,64]{2,1,0:T(8,128)(2,1)} %param.7) | copy-start | bytes 663556
  37.6 32.6 %collective-permute-start.2 = (bf16[64,4,1,256]{3,2,1,0:T(2,128)(2,1)}, bf16[64,4,1,256]{3,2,1,0:T(2,128)(2,1)S(1)}, u32[]{:S(2)}, u32[]{:S(2)}) collective-permute-start(bf16[64,4,1,256]{3,2,1,0:T(2,128)(2,1)} %get-tuple-element.266), channel_id=1, source_target_pairs={{0,1},{2,3},{4,5},{6,7},{8,9},{10,11},{12,13},{14,15},{16,17},{18,... | collective-permute-start | bytes 393224 | tf_op jit(solution)/shard_map/ppermute | solution.py:15
  41.8 28.4 %collective-permute-start.3 = (bf16[64,4,1,256]{3,2,1,0:T(2,128)(2,1)}, bf16[64,4,1,256]{3,2,1,0:T(2,128)(2,1)S(1)}, u32[]{:S(2)}, u32[]{:S(2)}) collective-permute-start(bf16[64,4,1,256]{3,2,1,0:T(2,128)(2,1)} %get-tuple-element.267), channel_id=1, source_target_pairs={{1,0},{3,2},{5,4},{7,6},{9,8},{11,10},{13,12},{15,14},{17,16},{19,... | collective-permute-start | bytes 393224 | tf_op jit(solution)/shard_map/ppermute | solution.py:17
  45.4 12.1 %copy-start.67 = (bf16[64,3,64]{2,0,1:T(8,128)(2,1)S(1)}, bf16[64,3,64]{2,0,1:T(8,128)(2,1)}, u32[]{:S(2)}) copy-start(bf16[64,3,64]{2,0,1:T(8,128)(2,1)} %get-tuple-element.223) | copy-start | bytes 73732
  45.4 12.9 %copy-start.66 = (bf16[64,3,64]{2,0,1:T(8,128)(2,1)S(1)}, bf16[64,3,64]{2,0,1:T(8,128)(2,1)}, u32[]{:S(2)}) copy-start(bf16[64,3,64]{2,0,1:T(8,128)(2,1)} %get-tuple-element.224) | copy-start | bytes 73732
  45.4 13.6 %copy-start.65 = (bf16[64,3,64]{2,0,1:T(8,128)(2,1)S(1)}, bf16[64,3,64]{2,0,1:T(8,128)(2,1)}, u32[]{:S(2)}) copy-start(bf16[64,3,64]{2,0,1:T(8,128)(2,1)} %get-tuple-element.225) | copy-start | bytes 73732
  45.4 14.3 %copy-start.64 = (bf16[64,3,64]{2,0,1:T(8,128)(2,1)S(1)}, bf16[64,3,64]{2,0,1:T(8,128)(2,1)}, u32[]{:S(2)}) copy-start(bf16[64,3,64]{2,0,1:T(8,128)(2,1)} %get-tuple-element.226) | copy-start | bytes 73732
  45.4 15.0 %copy-start.63 = (bf16[64,3,64]{2,0,1:T(8,128)(2,1)S(1)}, bf16[64,3,64]{2,0,1:T(8,128)(2,1)}, u32[]{:S(2)}) copy-start(bf16[64,3,64]{2,0,1:T(8,128)(2,1)} %get-tuple-element.227) | copy-start | bytes 73732
  45.4 15.7 %copy-start.62 = (bf16[64,3,64]{2,0,1:T(8,128)(2,1)S(1)}, bf16[64,3,64]{2,0,1:T(8,128)(2,1)}, u32[]{:S(2)}) copy-start(bf16[64,3,64]{2,0,1:T(8,128)(2,1)} %get-tuple-element.228) | copy-start | bytes 73732
  45.4 16.4 %copy-start.61 = (bf16[64,3,64]{2,0,1:T(8,128)(2,1)S(1)}, bf16[64,3,64]{2,0,1:T(8,128)(2,1)}, u32[]{:S(2)}) copy-start(bf16[64,3,64]{2,0,1:T(8,128)(2,1)} %get-tuple-element.229) | copy-start | bytes 73732
  45.4 17.1 %copy-start.60 = (bf16[64,3,64]{2,0,1:T(8,128)(2,1)S(1)}, bf16[64,3,64]{2,0,1:T(8,128)(2,1)}, u32[]{:S(2)}) copy-start(bf16[64,3,64]{2,0,1:T(8,128)(2,1)} %get-tuple-element.230) | copy-start | bytes 73732
  45.4 17.8 %copy-start.59 = (bf16[64,3,64]{2,0,1:T(8,128)(2,1)S(1)}, bf16[64,3,64]{2,0,1:T(8,128)(2,1)}, u32[]{:S(2)}) copy-start(bf16[64,3,64]{2,0,1:T(8,128)(2,1)} %get-tuple-element.231) | copy-start | bytes 73732
  45.5 18.5 %copy-start.58 = (bf16[3,64,64]{2,1,0:T(8,128)(2,1)S(1)}, bf16[3,64,64]{2,1,0:T(8,128)(2,1)}, u32[]{:S(2)}) copy-start(bf16[3,64,64]{2,1,0:T(8,128)(2,1)} %get-tuple-element.232) | copy-start | bytes 73732
  45.5 19.1 %copy-start.57 = (bf16[3,64,64]{2,1,0:T(8,128)(2,1)S(1)}, bf16[3,64,64]{2,1,0:T(8,128)(2,1)}, u32[]{:S(2)}) copy-start(bf16[3,64,64]{2,1,0:T(8,128)(2,1)} %get-tuple-element.233) | copy-start | bytes 73732
  45.5 19.7 %copy-start.56 = (bf16[3,64,64]{2,1,0:T(8,128)(2,1)S(1)}, bf16[3,64,64]{2,1,0:T(8,128)(2,1)}, u32[]{:S(2)}) copy-start(bf16[3,64,64]{2,1,0:T(8,128)(2,1)} %get-tuple-element.234) | copy-start | bytes 73732
  45.5 20.3 %copy-start.55 = (bf16[3,64,64]{2,1,0:T(8,128)(2,1)S(1)}, bf16[3,64,64]{2,1,0:T(8,128)(2,1)}, u32[]{:S(2)}) copy-start(bf16[3,64,64]{2,1,0:T(8,128)(2,1)} %get-tuple-element.235) | copy-start | bytes 73732
  45.5 20.9 %copy-start.54 = (bf16[3,64,64]{2,1,0:T(8,128)(2,1)S(1)}, bf16[3,64,64]{2,1,0:T(8,128)(2,1)}, u32[]{:S(2)}) copy-start(bf16[3,64,64]{2,1,0:T(8,128)(2,1)} %get-tuple-element.236) | copy-start | bytes 73732
  45.5 21.5 %copy-start.53 = (bf16[3,64,64]{2,1,0:T(8,128)(2,1)S(1)}, bf16[3,64,64]{2,1,0:T(8,128)(2,1)}, u32[]{:S(2)}) copy-start(bf16[3,64,64]{2,1,0:T(8,128)(2,1)} %get-tuple-element.237) | copy-start | bytes 73732
  45.5 22.1 %copy-start.52 = (bf16[3,64,64]{2,1,0:T(8,128)(2,1)S(1)}, bf16[3,64,64]{2,1,0:T(8,128)(2,1)}, u32[]{:S(2)}) copy-start(bf16[3,64,64]{2,1,0:T(8,128)(2,1)} %get-tuple-element.238) | copy-start | bytes 73732
  45.5 22.8 %copy-start.51 = (bf16[3,64,64]{2,1,0:T(8,128)(2,1)S(1)}, bf16[3,64,64]{2,1,0:T(8,128)(2,1)}, u32[]{:S(2)}) copy-start(bf16[3,64,64]{2,1,0:T(8,128)(2,1)} %get-tuple-element.239) | copy-start | bytes 73732
  84.3 3.9 %copy-start.33 = (bf16[64,1024]{1,0:T(8,128)(2,1)S(1)}, bf16[64,1024]{1,0:T(8,128)(2,1)}, u32[]{:S(2)}) copy-start(bf16[64,1024]{1,0:T(8,128)(2,1)} %reshape.794) | copy-start | bytes 393220
  84.4 3.9 %copy-start.32 = (bf16[64,1024]{1,0:T(8,128)(2,1)S(1)}, bf16[64,1024]{1,0:T(8,128)(2,1)}, u32[]{:S(2)}) copy-start(bf16[64,1024]{1,0:T(8,128)(2,1)} %reshape.798) | copy-start | bytes 393220
  85.2 3.1 copy-start.31
  91.7 14.6 %copy-start.91 = (bf16[3,128,64]{1,2,0:T(8,128)(2,1)S(1)}, bf16[3,128,64]{1,2,0:T(8,128)(2,1)}, u32[]{:S(2)}) copy-start(bf16[3,128,64]{1,2,0:T(8,128)(2,1)} %copy.145) | copy-start | bytes 147460
  91.7 14.7 %copy-start.42 = (bf16[3,128,64]{1,2,0:T(8,128)(2,1)S(1)}, bf16[3,128,64]{1,2,0:T(8,128)(2,1)}, u32[]{:S(2)}) copy-start(bf16[3,128,64]{1,2,0:T(8,128)(2,1)} %copy.146) | copy-start | bytes 147460
  91.7 15.0 %copy-start.41 = (bf16[3,128,64]{1,2,0:T(8,128)(2,1)S(1)}, bf16[3,128,64]{1,2,0:T(8,128)(2,1)}, u32[]{:S(2)}) copy-start(bf16[3,128,64]{1,2,0:T(8,128)(2,1)} %copy.147) | copy-start | bytes 147460
  92.7 14.2 %copy-start.40 = (bf16[3,128,64]{1,2,0:T(8,128)(2,1)S(1)}, bf16[3,128,64]{1,2,0:T(8,128)(2,1)}, u32[]{:S(2)}) copy-start(bf16[3,128,64]{1,2,0:T(8,128)(2,1)} %copy.148) | copy-start | bytes 147460
  92.7 14.4 %copy-start.39 = (bf16[3,128,64]{1,2,0:T(8,128)(2,1)S(1)}, bf16[3,128,64]{1,2,0:T(8,128)(2,1)}, u32[]{:S(2)}) copy-start(bf16[3,128,64]{1,2,0:T(8,128)(2,1)} %copy.149) | copy-start | bytes 147460
  92.7 14.6 %copy-start.38 = (bf16[3,128,64]{1,2,0:T(8,128)(2,1)S(1)}, bf16[3,128,64]{1,2,0:T(8,128)(2,1)}, u32[]{:S(2)}) copy-start(bf16[3,128,64]{1,2,0:T(8,128)(2,1)} %copy.150) | copy-start | bytes 147460
  92.7 14.8 %copy-start.37 = (bf16[3,128,64]{1,2,0:T(8,128)(2,1)S(1)}, bf16[3,128,64]{1,2,0:T(8,128)(2,1)}, u32[]{:S(2)}) copy-start(bf16[3,128,64]{1,2,0:T(8,128)(2,1)} %copy.151) | copy-start | bytes 147460
  93.1 14.8 %copy-start.90 = (bf16[3,128,64]{1,2,0:T(8,128)(2,1)S(1)}, bf16[3,128,64]{1,2,0:T(8,128)(2,1)}, u32[]{:S(2)}) copy-start(bf16[3,128,64]{1,2,0:T(8,128)(2,1)} %copy.153) | copy-start | bytes 147460
  93.1 5.2 %collective-permute-start.5 = (bf16[64,1,1,128]{3,0,2,1:T(8,128)(2,1)S(1)}, bf16[64,1,1,128]{3,0,2,1:T(8,128)(2,1)S(1)}, u32[]{:S(2)}, u32[]{:S(2)}) collective-permute-start(bf16[64,1,1,128]{3,0,2,1:T(8,128)(2,1)S(1)} %fusion.245), channel_id=1, source_target_pairs={{2,0},{4,2},{6,4},{8,6},{10,8},{12,10},{14,12},{16,14},{18,16},{20... | collective-permute-start | bytes 49160 | tf_op jit(solution)/shard_map/ppermute | solution.py:17
  94.4 3.9 %collective-permute-start.4 = (bf16[64,1,1,128]{3,0,2,1:T(8,128)(2,1)S(1)}, bf16[64,1,1,128]{3,0,2,1:T(8,128)(2,1)S(1)}, u32[]{:S(2)}, u32[]{:S(2)}) collective-permute-start(bf16[64,1,1,128]{3,0,2,1:T(8,128)(2,1)S(1)} %fusion.245), channel_id=1, source_target_pairs={{0,2},{2,4},{4,6},{6,8},{8,10},{10,12},{12,14},{14,16},{16,18},{18... | collective-permute-start | bytes 49160 | tf_op jit(solution)/shard_map/ppermute | solution.py:15
  98.4 6.1 %collective-permute-start.7 = (bf16[64,3,1,128]{3,0,2,1:T(8,128)(2,1)S(1)}, bf16[64,3,1,128]{3,0,2,1:T(8,128)(2,1)S(1)}, u32[]{:S(2)}, u32[]{:S(2)}) collective-permute-start(bf16[64,3,1,128]{3,0,2,1:T(8,128)(2,1)S(1)} %pad_maximum_fusion.18), channel_id=1, source_target_pairs={{1,0},{3,2},{5,4},{7,6},{9,8},{11,10},{13,12},{15,14},{17,16},{19,... | collective-permute-start | bytes 147464 | tf_op jit(solution)/shard_map/ppermute | solution.py:17
  99.7 6.3 %collective-permute-start.6 = (bf16[64,3,1,128]{3,0,2,1:T(8,128)(2,1)S(1)}, bf16[64,3,1,128]{3,0,2,1:T(8,128)(2,1)S(1)}, u32[]{:S(2)}, u32[]{:S(2)}) collective-permute-start(bf16[64,3,1,128]{3,0,2,1:T(8,128)(2,1)S(1)} %pad_maximum_fusion.18), channel_id=1, source_target_pairs={{0,1},{2,3},{4,5},{6,7},{8,9},{10,11},{12,13},{14,15},{16,17},{18,... | collective-permute-start | bytes 147464 | tf_op jit(solution)/shard_map/ppermute | solution.py:15
  106.2 3.2 %copy-start.74 = (bf16[64,128]{1,0:T(8,128)(2,1)}, bf16[64,128]{1,0:T(8,128)(2,1)S(1)}, u32[]{:S(2)}) copy-start(bf16[64,128]{1,0:T(8,128)(2,1)S(1)} %get-tuple-element.240) | copy-start | bytes 49156
  106.3 3.2 %copy-start.76 = (bf16[64,128]{1,0:T(8,128)(2,1)}, bf16[64,128]{1,0:T(8,128)(2,1)S(1)}, u32[]{:S(2)}) copy-start(bf16[64,128]{1,0:T(8,128)(2,1)S(1)} %get-tuple-element.257) | copy-start | bytes 49156
  106.7 8.5 %copy-start.78 = (bf16[64,128]{1,0:T(8,128)(2,1)}, bf16[64,128]{1,0:T(8,128)(2,1)S(1)}, u32[]{:S(2)}) copy-start(bf16[64,128]{1,0:T(8,128)(2,1)S(1)} %get-tuple-element.280) | copy-start | bytes 49156
  108.2 20.6 %collective-permute-start.9 = (bf16[128,1,1,128]{0,3,2,1:T(8,128)(2,1)S(1)}, bf16[128,1,1,128]{0,3,2,1:T(8,128)(2,1)S(1)}, u32[]{:S(2)}, u32[]{:S(2)}) collective-permute-start(bf16[128,1,1,128]{0,3,2,1:T(8,128)(2,1)S(1)} %bitcast.408), channel_id=1, source_target_pairs={{2,0},{4,2},{6,4},{8,6},{10,8},{12,10},{14,12},{16,14},{18,16},{20... | collective-permute-start | bytes 98312 | tf_op jit(solution)/shard_map/ppermute | solution.py:17
  109.5 19.3 %collective-permute-start.8 = (bf16[128,1,1,128]{0,3,2,1:T(8,128)(2,1)S(1)}, bf16[128,1,1,128]{0,3,2,1:T(8,128)(2,1)S(1)}, u32[]{:S(2)}, u32[]{:S(2)}) collective-permute-start(bf16[128,1,1,128]{0,3,2,1:T(8,128)(2,1)S(1)} %bitcast.409), channel_id=1, source_target_pairs={{0,2},{2,4},{4,6},{6,8},{8,10},{10,12},{12,14},{14,16},{16,18},{18... | collective-permute-start | bytes 98312 | tf_op jit(solution)/shard_map/ppermute | solution.py:15
  115.9 18.9 %all-to-all-start = ((bf16[2,2,4096]{2,1,0:T(2,128)(2,1)}), bf16[2,2,4096]{2,1,0:T(2,128)(2,1)S(1)}, u32[]{:S(2)}, u32[]{:S(2)}) async-start(bf16[2,2,4096]{2,1,0:T(2,128)(2,1)} %reshape.942), calls=%async_computation | async-start | bytes 65536 | tf_op jit(solution)/shard_map/all_to_all | solution.py:129
  119.2 187.0 %all-reduce.7.cloned.1.call-start = ((), (), s32[]{:S(2)}) async-start(), calls=%async_computation.2 | async-start | bytes 5308416 | tf_op jit(solution)/shard_map/psum | solution.py:155
  122.9 5.6 %copy-start.75 = (bf16[64,128]{1,0:T(8,128)(2,1)S(1)}, bf16[64,128]{1,0:T(8,128)(2,1)}, u32[]{:S(2)}) copy-start(bf16[64,128]{1,0:T(8,128)(2,1)} %copy-done.74) | copy-start | bytes 49156
  122.9 5.6 %copy-start.77 = (bf16[64,128]{1,0:T(8,128)(2,1)S(1)}, bf16[64,128]{1,0:T(8,128)(2,1)}, u32[]{:S(2)}) copy-start(bf16[64,128]{1,0:T(8,128)(2,1)} %copy-done.76) | copy-start | bytes 49156
  122.9 5.6 %copy-start.79 = (bf16[64,128]{1,0:T(8,128)(2,1)S(1)}, bf16[64,128]{1,0:T(8,128)(2,1)}, u32[]{:S(2)}) copy-start(bf16[64,128]{1,0:T(8,128)(2,1)} %copy-done.78) | copy-start | bytes 49156
  128.8 6.7 %collective-permute-start.11 = (bf16[128,3,1,128]{0,3,2,1:T(8,128)(2,1)S(1)}, bf16[128,3,1,128]{0,3,2,1:T(8,128)(2,1)S(1)}, u32[]{:S(2)}, u32[]{:S(2)}) collective-permute-start(bf16[128,3,1,128]{0,3,2,1:T(8,128)(2,1)S(1)} %pad_maximum_fusion.17), channel_id=1, source_target_pairs={{1,0},{3,2},{5,4},{7,6},{9,8},{11,10},{13,12},{15,14},{17,16},{19,... | collective-permute-start | bytes 294920 | tf_op jit(solution)/shard_map/ppermute | solution.py:17
  130.1 6.8 %collective-permute-start.10 = (bf16[128,3,1,128]{0,3,2,1:T(8,128)(2,1)S(1)}, bf16[128,3,1,128]{0,3,2,1:T(8,128)(2,1)S(1)}, u32[]{:S(2)}, u32[]{:S(2)}) collective-permute-start(bf16[128,3,1,128]{0,3,2,1:T(8,128)(2,1)S(1)} %pad_maximum_fusion.17), channel_id=1, source_target_pairs={{0,1},{2,3},{4,5},{6,7},{8,9},{10,11},{12,13},{14,15},{16,17},{18,... | collective-permute-start | bytes 294920 | tf_op jit(solution)/shard_map/ppermute | solution.py:15
  134.7 2.7 copy-start
  137.4 6.9 %copy-start.36 = (f32[64,1024]{1,0:T(8,128)S(1)}, f32[64,1024]{1,0:T(8,128)}, u32[]{:S(2)}) copy-start(f32[64,1024]{1,0:T(8,128)} %get-tuple-element.287) | copy-start | bytes 786436
  147.0 6.7 %collective-permute-start.13 = (bf16[64,1,2,256]{3,2,1,0:T(2,128)(2,1)S(1)}, bf16[64,1,2,256]{3,2,1,0:T(2,128)(2,1)S(1)}, u32[]{:S(2)}, u32[]{:S(2)}) collective-permute-start(bf16[64,1,2,256]{3,2,1,0:T(2,128)(2,1)S(1)} %get-tuple-element.271), channel_id=1, source_target_pairs={{2,0},{4,2},{6,4},{8,6},{10,8},{12,10},{14,12},{16,14},{18,16},{20... | collective-permute-start | bytes 196616 | tf_op jit(solution)/shard_map/ppermute | solution.py:17
  148.3 5.4 %collective-permute-start.12 = (bf16[64,1,2,256]{3,2,1,0:T(2,128)(2,1)S(1)}, bf16[64,1,2,256]{3,2,1,0:T(2,128)(2,1)S(1)}, u32[]{:S(2)}, u32[]{:S(2)}) collective-permute-start(bf16[64,1,2,256]{3,2,1,0:T(2,128)(2,1)S(1)} %get-tuple-element.272), channel_id=1, source_target_pairs={{0,2},{2,4},{4,6},{6,8},{8,10},{10,12},{12,14},{14,16},{16,18},{18... | collective-permute-start | bytes 196616 | tf_op jit(solution)/shard_map/ppermute | solution.py:15
  154.6 9.0 %collective-permute-start.14 = (bf16[64,4,1,256]{3,2,1,0:T(2,128)(2,1)S(1)}, bf16[64,4,1,256]{3,2,1,0:T(2,128)(2,1)S(1)}, u32[]{:S(2)}, u32[]{:S(2)}) collective-permute-start(bf16[64,4,1,256]{3,2,1,0:T(2,128)(2,1)S(1)} %get-tuple-element.261), channel_id=1, source_target_pairs={{0,1},{2,3},{4,5},{6,7},{8,9},{10,11},{12,13},{14,15},{16,17},{18,... | collective-permute-start | bytes 393224 | tf_op jit(solution)/shard_map/ppermute | solution.py:15
  158.6 9.7 %collective-permute-start.15 = (bf16[64,4,1,256]{3,2,1,0:T(2,128)(2,1)S(1)}, bf16[64,4,1,256]{3,2,1,0:T(2,128)(2,1)S(1)}, u32[]{:S(2)}, u32[]{:S(2)}) collective-permute-start(bf16[64,4,1,256]{3,2,1,0:T(2,128)(2,1)S(1)} %get-tuple-element.262), channel_id=1, source_target_pairs={{1,0},{3,2},{5,4},{7,6},{9,8},{11,10},{13,12},{15,14},{17,16},{19,... | collective-permute-start | bytes 393224 | tf_op jit(solution)/shard_map/ppermute | solution.py:17
  178.1 3.7 %copy-start.70 = (bf16[64,1024]{1,0:T(8,128)(2,1)S(1)}, bf16[64,1024]{1,0:T(8,128)(2,1)}, u32[]{:S(2)}) copy-start(bf16[64,1024]{1,0:T(8,128)(2,1)} %reshape.850) | copy-start | bytes 393220
  178.1 3.7 %copy-start.88 = (bf16[3,64,64]{2,1,0:T(8,128)(2,1)S(1)}, bf16[3,64,64]{2,1,0:T(8,128)(2,1)}, u32[]{:S(2)}) copy-start(bf16[3,64,64]{2,1,0:T(8,128)(2,1)} %rev.90) | copy-start | bytes 73732
  179.1 3.9 %copy-start.87 = (bf16[3,64,64]{2,1,0:T(8,128)(2,1)S(1)}, bf16[3,64,64]{2,1,0:T(8,128)(2,1)}, u32[]{:S(2)}) copy-start(bf16[3,64,64]{2,1,0:T(8,128)(2,1)} %rev.91) | copy-start | bytes 73732
  179.4 3.8 %copy-start.68 = (bf16[64,1024]{1,0:T(8,128)(2,1)S(1)}, bf16[64,1024]{1,0:T(8,128)(2,1)}, u32[]{:S(2)}) copy-start(bf16[64,1024]{1,0:T(8,128)(2,1)} %reshape.858) | copy-start | bytes 393220
  179.4 3.8 %copy-start.86 = (bf16[3,64,64]{2,1,0:T(8,128)(2,1)S(1)}, bf16[3,64,64]{2,1,0:T(8,128)(2,1)}, u32[]{:S(2)}) copy-start(bf16[3,64,64]{2,1,0:T(8,128)(2,1)} %rev.92) | copy-start | bytes 73732
  180.2 2.8 copy-start.72
  306.2 2.6 copy-start.34
  (50 other events, 67.9 us)
Sparse Core Ops, SparseCore 0:
  161.2 144.9 all-reduce.6
where the time goes:
time: 318 us; the launch traced here: 317 us
  waiting for transfers between devices  131 us (41%)
  local copies, waits for them, and re-layouts  75.2 us (24%)
  starting transfers between devices  49.8 us (16%)
  between operations  16.3 us (5%)
  blocking collectives  15.2 us (5%)
  matrix products  14.6 us (5%)
  other arithmetic  14.5 us (5%)
    psum x1, waiting for transfers between devices, local(): lax.psum(conv_weights(first_down, padded_in, fine_shape), ('space', 'filt'))  120 us
    ppermute x8, starting transfers between devices, extended(): lax.ppermute(tail, axis, [(i, (i + 1) % count) for i in range(ends)])  31.4 us
    unnamed x237, local copies, waits for them, and re-layouts  25.8 us
    reshape x58, local copies, waits for them, and re-layouts, window(): return section.reshape(padded.shape[0], extent_x * extent_y * extent_z)  17.6 us
    all_gather x1, blocking collectives, local(): whole_weight = lax.all_gather(second_weight, 'filt', axis=1, tiled=True)  15.2 us
    ppermute x8, starting transfers between devices, extended(): lax.ppermute(head, axis, [((i + 1) % count, i) for i in range(ends)])  10.8 us
    concatenate x10, other arithmetic, extended(): jnp.concatenate([lax.ppermute(tail, axis, [(i, (i + 1) % count) for i in...  9.21 us
    rev x27, local copies, waits for them, and re-layouts, conv_transpose(): tap_block = weight[24 - tap_base:27 - tap_base][::-1]  6.46 us
  transfers between devices with their start and end apart: 19, of which 6 were waited for; matrix products, arithmetic and copies ran while one was open for 27% of the time, Pallas kernels for 0%

commit v1 on v0

--- a/solution.py
+++ b/solution.py
@@ -152,7 +152,10 @@
     hidden_grad = spread_cells(pool_grad.reshape((channels,) + brick_shape))
     first_down = (hidden_grad.reshape(channels, -1) * silu_slope(first_pre)).astype(jnp.bfloat16)
     first_grad = (
-        lax.psum(conv_weights(first_down, padded_in, fine_shape), ("space", "filt")) * fine_scale
+        lax.psum(
+            lax.psum(conv_weights(first_down, padded_in, fine_shape), axis_name="filt"), "space"
+        )
+        * fine_scale
     )
     padded_back = pad_depth(
         extended(first_down.reshape((channels,) + fine_shape), (("space", 1), ("filt", 2)), 1)

time: 318 us -> 456 us (1.43)
  waiting for transfers between devices: 131 us -> 258 us
    psum x1 -> x3, waiting for transfers between devices: 120 us -> 247 us  [the longest x1 137 us: local(): lax.psum(conv_weights(down_grad, padded_pool, brick_shape), ('space', 'fi...]
    unnamed x237 -> x221, local copies, waits for them, and re-layouts: 25.8 us -> 24.8 us
  transfers between devices with their start and end apart: 19 -> 21, of which waited for: 6 -> 7; matrix products, arithmetic and copies ran while one was open for 27% -> 23% of each run, Pallas kernels for 0% -> 0%
where the time goes in v1:
time: 456 us; the launch traced here: 455 us
  waiting for transfers between devices  258 us (57%)
  local copies, waits for them, and re-layouts  78.3 us (17%)
  starting transfers between devices  50.5 us (11%)
  other arithmetic  18.1 us (4%)
  matrix products  18 us (4%)
  between operations  16 us (4%)
  blocking collectives  15.2 us (3%)
    psum x1, waiting for transfers between devices, local(): lax.psum(conv_weights(down_grad, padded_pool, brick_shape), ('space', 'fi...  137 us
    psum x1, waiting for transfers between devices, local(): lax.psum(lax.psum(conv_weights(first_down, padded_in, fine_shape), axis_n...  94.5 us
    ppermute x8, starting transfers between devices, extended(): lax.ppermute(tail, axis, [(i, (i + 1) % count) for i in range(ends)])  31.5 us
    unnamed x221, local copies, waits for them, and re-layouts  24.8 us
    reshape x58, local copies, waits for them, and re-layouts, window(): return section.reshape(padded.shape[0], extent_x * extent_y * extent_z)  18.2 us
    all_gather x1, blocking collectives, local(): whole_weight = lax.all_gather(second_weight, 'filt', axis=1, tiled=True)  15.2 us
    psum x1, waiting for transfers between devices, local(): lax.psum(conv_weights(first_down, padded_in, fine_shape), axis_name='filt')  15.1 us
    concatenate x10, other arithmetic, extended(): jnp.concatenate([lax.ppermute(tail, axis, [(i, (i + 1) % count) for i in...  10.7 us
  transfers between devices with their start and end apart: 21, of which 7 were waited for; matrix products, arithmetic and copies ran while one was open for 23% of the time, Pallas kernels for 0%

profile of v1, /device:TPU:0, one launch (start us, length us, event | category | flops | bytes accessed | tf_op | source)
XLA Modules:
  0.0 454.6 jit_solution(16171870684719389689)
XLA Ops:
  7.2 1.4 copy.107
  8.5 4.2 all-to-all-start.1
  12.8 1.0 fusion.162
  13.7 1.3 collective-permute-start.1
  15.0 3.0 collective-permute-start
  18.1 1.3 copy.96
  19.4 15.2 %all_gather.3 = bf16[27,128,64]{2,0,1:T(8,128)(2,1)S(1)} all-gather(bf16[27,64,64]{2,0,1:T(8,128)(2,1)S(1)} %copy.96), channel_id=1, replica_groups=mesh['space'=16,'filt'=2] {'filt'}, dimensions={1}, use_global_device_ids=true | all-gather | bytes 663552 | tf_op jit(solution)/shard_map/all_gather | solution.py:124
  34.6 1.3 fusion.155
  36.4 1.2 fusion.160
  37.6 4.2 collective-permute-start.2
  41.8 1.5 collective-permute-start.3
  43.3 0.9 fusion.158
  45.5 1.8 copy.153
  47.3 1.0 copy.152
  48.3 1.6 copy.151
  49.9 1.6 copy.150
  51.5 1.6 copy.149
  56.0 1.4 rev.98
  70.2 1.7 pad_maximum_fusion.9
  75.6 2.4 select_maximum_fusion.2
  78.0 2.9 fusion.157
  89.7 1.1 constant_dynamic-update-slice_fusion.29
  90.9 1.2 fusion.163
  95.2 0.9 multiply_convert_fusion.1
  96.6 1.3 collective-permute-start.5
  97.9 3.0 collective-permute-start.4
  101.8 1.3 collective-permute-start.7
  103.1 4.8 %collective-permute-start.6 = (bf16[64,3,1,128]{3,0,2,1:T(8,128)(2,1)S(1)}, bf16[64,3,1,128]{3,0,2,1:T(8,128)(2,1)S(1)}, u32[]{:S(2)}, u32[]{:S(2)}) collective-permute-start(bf16[64,3,1,128]{3,0,2,1:T(8,128)(2,1)S(1)} %pad_maximum_fusion.18), channel_id=1, source_target_pairs={{0,1},{2,3},{4,5},{6,7},{8,9},{10,11},{12,13},{14,15},{16,17},{18,... | collective-permute-start | bytes 147464 | tf_op jit(solution)/shard_map/ppermute | solution.py:15
  107.9 1.5 collective-permute-done.6
  111.6 1.3 collective-permute-start.9
  112.9 3.9 collective-permute-start.8
  122.4 3.9 all-to-all-start
  126.9 1.0 copy.126
  127.9 1.7 copy.125
  129.6 1.7 copy.124
  131.3 1.7 copy.123
  133.0 0.9 bitcast_dynamic-update-slice_fusion.8
  134.0 0.9 bitcast_dynamic-update-slice_fusion.7
  134.9 0.9 bitcast_dynamic-update-slice_fusion.6
  136.0 1.2 copy-done
  138.0 1.3 collective-permute-start.11
  139.3 4.6 %collective-permute-start.10 = (bf16[128,3,1,128]{0,3,2,1:T(8,128)(2,1)S(1)}, bf16[128,3,1,128]{0,3,2,1:T(8,128)(2,1)S(1)}, u32[]{:S(2)}, u32[]{:S(2)}) collective-permute-start(bf16[128,3,1,128]{0,3,2,1:T(8,128)(2,1)S(1)} %pad_maximum_fusion.17), channel_id=1, source_target_pairs={{0,1},{2,3},{4,5},{6,7},{8,9},{10,11},{12,13},{14,15},{16,17},{18,... | collective-permute-start | bytes 294920 | tf_op jit(solution)/shard_map/ppermute | solution.py:15
  144.0 0.8 copy.131
  144.8 1.2 collective-permute-done.10
  147.3 5.5 %while.14 = (s32[]{:T(128)}, f32[64,128]{1,0:T(8,128)}, bf16[27,128,64]{2,1,0:T(8,128)(2,1)S(1)}, bf16[128,3,3,130]{3,0,2,1:T(8,128)(2,1)S(1)}, s32[]{:T(128)}, ...) while((s32[]{:T(128)}, f32[64,128]{1,0:T(8,128)}, ...), condition=%wide.region_2.3_spmd.clone, body=%wide.region_1.2_spmd.clone.sunk | while | flops 29736976 | bytes 3318213 | solution.py:149
  152.8 0.8 broadcast_multiply_fusion.1
  154.0 1.1 multiply_convert_fusion
  157.7 1.3 collective-permute-start.13
  159.0 3.9 collective-permute-start.12
  163.1 0.9 copy-done.12
  164.9 4.0 collective-permute-start.14
  169.0 1.3 collective-permute-start.15
  172.9 1.6 collective-permute-done.14
  174.6 7.1 %collective-permute-done.15 = bf16[64,4,1,256]{3,2,1,0:T(2,128)(2,1)S(1)} collective-permute-done((bf16[64,4,1,256]{3,2,1,0:T(2,128)(2,1)S(1)}, bf16[64,4,1,256]{3,2,1,0:T(2,128)(2,1)S(1)}, u32[]{:S(2)}, u32[]{:S(2)}) %collective-permute-start.15) | collective-permute-done | bytes 131104 | tf_op jit(solution)/shard_map/ppermute | solution.py:17
  181.7 1.7 pad_maximum_fusion.1
  185.2 2.4 select_maximum_fusion
  187.6 2.9 fusion.156
  192.8 1.0 convolution_add_fusion.15
  195.6 15.1 %all-reduce.8.cloned.1.call-done = f32[27,64,64]{1,2,0:T(8,128)} async-done(((f32[27,64,64]{1,2,0:T(8,128)}), f32[27,64,64]{1,2,0:T(8,128)}) %all-reduce.8.cloned.1.call-update) | async-done | bytes 442384 | tf_op jit(solution)/shard_map/psum | solution.py:156
  211.7 137.2 %all-reduce.12.cloned.1.call-done = f32[27,128,64]{2,1,0:T(8,128)} async-done(((f32[27,128,64]{2,1,0:T(8,128)}), f32[27,128,64]{2,1,0:T(8,128)}) %all-reduce.12.cloned.1.call-update) | async-done | bytes 884752 | tf_op jit(solution)/shard_map/psum | solution.py:134
  348.8 2.2 dynamic-slice_multiply_fusion
  351.0 94.5 %all-reduce.10.cloned.1.call-done = f32[27,64,64]{1,2,0:T(8,128)} async-done(((f32[27,64,64]{1,2,0:T(8,128)}), f32[27,64,64]{1,2,0:T(8,128)}) %all-reduce.10.cloned.1.call-update) | async-done | bytes 442384 | tf_op jit(solution)/shard_map/psum | solution.py:155
  445.5 1.3 broadcast_multiply_fusion
  446.8 1.2 copy.133
  (433 shorter events, 61.9 us)
Async XLA Ops:
  8.5 92.4 %all-to-all-start.1 = ((bf16[64,1,2,128]{3,0,1,2:T(8,128)(2,1)}), bf16[64,1,2,128]{3,0,1,2:T(8,128)(2,1)}, u32[]{:S(2)}, u32[]{:S(2)}) async-start(bf16[64,1,2,128]{3,0,1,2:T(8,128)(2,1)} %copy.107), calls=%async_computation.1 | async-start | bytes 65536 | tf_op jit(solution)/shard_map/all_to_all | solution.py:130
  13.7 22.2 %collective-permute-start.1 = (bf16[64,1,2,256]{3,2,1,0:T(2,128)(2,1)S(1)}, bf16[64,1,2,256]{3,2,1,0:T(2,128)(2,1)S(1)}, u32[]{:S(2)}, u32[]{:S(2)}) collective-permute-start(bf16[64,1,2,256]{3,2,1,0:T(2,128)(2,1)S(1)} %get-tuple-element.274), channel_id=1, source_target_pairs={{2,0},{4,2},{6,4},{8,6},{10,8},{12,10},{14,12},{16,14},{18,16},{20... | collective-permute-start | bytes 196616 | tf_op jit(solution)/shard_map/ppermute | solution.py:17
  15.0 20.9 %collective-permute-start = (bf16[64,1,2,256]{3,2,1,0:T(2,128)(2,1)S(1)}, bf16[64,1,2,256]{3,2,1,0:T(2,128)(2,1)S(1)}, u32[]{:S(2)}, u32[]{:S(2)}) collective-permute-start(bf16[64,1,2,256]{3,2,1,0:T(2,128)(2,1)S(1)} %get-tuple-element.275), channel_id=1, source_target_pairs={{0,2},{2,4},{4,6},{6,8},{8,10},{10,12},{12,14},{14,16},{16,18},{18... | collective-permute-start | bytes 196616 | tf_op jit(solution)/shard_map/ppermute | solution.py:15
  19.4 16.6 %copy-start.9 = (bf16[64,2,2,256]{3,2,1,0:T(2,128)(2,1)S(1)}, bf16[64,2,2,256]{3,2,1,0:T(2,128)(2,1)}, u32[]{:S(2)}) copy-start(bf16[64,2,2,256]{3,2,1,0:T(2,128)(2,1)} %param.6) | copy-start | bytes 393220
  34.6 8.6 %copy-start.33 = (bf16[27,64,64]{2,1,0:T(8,128)(2,1)S(1)}, bf16[27,64,64]{2,1,0:T(8,128)(2,1)}, u32[]{:S(2)}) copy-start(bf16[27,64,64]{2,1,0:T(8,128)(2,1)} %param.7) | copy-start | bytes 663556
  37.6 32.6 %collective-permute-start.2 = (bf16[64,4,1,256]{3,2,1,0:T(2,128)(2,1)}, bf16[64,4,1,256]{3,2,1,0:T(2,128)(2,1)S(1)}, u32[]{:S(2)}, u32[]{:S(2)}) collective-permute-start(bf16[64,4,1,256]{3,2,1,0:T(2,128)(2,1)} %get-tuple-element.264), channel_id=1, source_target_pairs={{0,1},{2,3},{4,5},{6,7},{8,9},{10,11},{12,13},{14,15},{16,17},{18,... | collective-permute-start | bytes 393224 | tf_op jit(solution)/shard_map/ppermute | solution.py:15
  41.8 28.4 %collective-permute-start.3 = (bf16[64,4,1,256]{3,2,1,0:T(2,128)(2,1)}, bf16[64,4,1,256]{3,2,1,0:T(2,128)(2,1)S(1)}, u32[]{:S(2)}, u32[]{:S(2)}) collective-permute-start(bf16[64,4,1,256]{3,2,1,0:T(2,128)(2,1)} %get-tuple-element.265), channel_id=1, source_target_pairs={{1,0},{3,2},{5,4},{7,6},{9,8},{11,10},{13,12},{15,14},{17,16},{19,... | collective-permute-start | bytes 393224 | tf_op jit(solution)/shard_map/ppermute | solution.py:17
  45.3 12.1 %copy-start.63 = (bf16[64,3,64]{2,0,1:T(8,128)(2,1)S(1)}, bf16[64,3,64]{2,0,1:T(8,128)(2,1)}, u32[]{:S(2)}) copy-start(bf16[64,3,64]{2,0,1:T(8,128)(2,1)} %get-tuple-element.221) | copy-start | bytes 73732
  45.3 12.8 %copy-start.62 = (bf16[64,3,64]{2,0,1:T(8,128)(2,1)S(1)}, bf16[64,3,64]{2,0,1:T(8,128)(2,1)}, u32[]{:S(2)}) copy-start(bf16[64,3,64]{2,0,1:T(8,128)(2,1)} %get-tuple-element.222) | copy-start | bytes 73732
  45.3 13.5 %copy-start.61 = (bf16[64,3,64]{2,0,1:T(8,128)(2,1)S(1)}, bf16[64,3,64]{2,0,1:T(8,128)(2,1)}, u32[]{:S(2)}) copy-start(bf16[64,3,64]{2,0,1:T(8,128)(2,1)} %get-tuple-element.223) | copy-start | bytes 73732
  45.3 14.3 %copy-start.60 = (bf16[64,3,64]{2,0,1:T(8,128)(2,1)S(1)}, bf16[64,3,64]{2,0,1:T(8,128)(2,1)}, u32[]{:S(2)}) copy-start(bf16[64,3,64]{2,0,1:T(8,128)(2,1)} %get-tuple-element.224) | copy-start | bytes 73732
  45.3 15.0 %copy-start.59 = (bf16[64,3,64]{2,0,1:T(8,128)(2,1)S(1)}, bf16[64,3,64]{2,0,1:T(8,128)(2,1)}, u32[]{:S(2)}) copy-start(bf16[64,3,64]{2,0,1:T(8,128)(2,1)} %get-tuple-element.225) | copy-start | bytes 73732
  45.4 15.7 %copy-start.58 = (bf16[64,3,64]{2,0,1:T(8,128)(2,1)S(1)}, bf16[64,3,64]{2,0,1:T(8,128)(2,1)}, u32[]{:S(2)}) copy-start(bf16[64,3,64]{2,0,1:T(8,128)(2,1)} %get-tuple-element.226) | copy-start | bytes 73732
  45.4 16.4 %copy-start.57 = (bf16[64,3,64]{2,0,1:T(8,128)(2,1)S(1)}, bf16[64,3,64]{2,0,1:T(8,128)(2,1)}, u32[]{:S(2)}) copy-start(bf16[64,3,64]{2,0,1:T(8,128)(2,1)} %get-tuple-element.227) | copy-start | bytes 73732
  45.4 17.1 %copy-start.56 = (bf16[64,3,64]{2,0,1:T(8,128)(2,1)S(1)}, bf16[64,3,64]{2,0,1:T(8,128)(2,1)}, u32[]{:S(2)}) copy-start(bf16[64,3,64]{2,0,1:T(8,128)(2,1)} %get-tuple-element.228) | copy-start | bytes 73732
  45.4 17.8 %copy-start.55 = (bf16[64,3,64]{2,0,1:T(8,128)(2,1)S(1)}, bf16[64,3,64]{2,0,1:T(8,128)(2,1)}, u32[]{:S(2)}) copy-start(bf16[64,3,64]{2,0,1:T(8,128)(2,1)} %get-tuple-element.229) | copy-start | bytes 73732
  45.4 18.5 %copy-start.54 = (bf16[3,64,64]{2,1,0:T(8,128)(2,1)S(1)}, bf16[3,64,64]{2,1,0:T(8,128)(2,1)}, u32[]{:S(2)}) copy-start(bf16[3,64,64]{2,1,0:T(8,128)(2,1)} %get-tuple-element.230) | copy-start | bytes 73732
  45.4 19.1 %copy-start.53 = (bf16[3,64,64]{2,1,0:T(8,128)(2,1)S(1)}, bf16[3,64,64]{2,1,0:T(8,128)(2,1)}, u32[]{:S(2)}) copy-start(bf16[3,64,64]{2,1,0:T(8,128)(2,1)} %get-tuple-element.231) | copy-start | bytes 73732
  45.4 19.7 %copy-start.52 = (bf16[3,64,64]{2,1,0:T(8,128)(2,1)S(1)}, bf16[3,64,64]{2,1,0:T(8,128)(2,1)}, u32[]{:S(2)}) copy-start(bf16[3,64,64]{2,1,0:T(8,128)(2,1)} %get-tuple-element.232) | copy-start | bytes 73732
  45.4 20.3 %copy-start.51 = (bf16[3,64,64]{2,1,0:T(8,128)(2,1)S(1)}, bf16[3,64,64]{2,1,0:T(8,128)(2,1)}, u32[]{:S(2)}) copy-start(bf16[3,64,64]{2,1,0:T(8,128)(2,1)} %get-tuple-element.233) | copy-start | bytes 73732
  45.4 20.9 %copy-start.50 = (bf16[3,64,64]{2,1,0:T(8,128)(2,1)S(1)}, bf16[3,64,64]{2,1,0:T(8,128)(2,1)}, u32[]{:S(2)}) copy-start(bf16[3,64,64]{2,1,0:T(8,128)(2,1)} %get-tuple-element.234) | copy-start | bytes 73732
  45.4 21.5 %copy-start.49 = (bf16[3,64,64]{2,1,0:T(8,128)(2,1)S(1)}, bf16[3,64,64]{2,1,0:T(8,128)(2,1)}, u32[]{:S(2)}) copy-start(bf16[3,64,64]{2,1,0:T(8,128)(2,1)} %get-tuple-element.235) | copy-start | bytes 73732
  45.5 22.1 %copy-start.48 = (bf16[3,64,64]{2,1,0:T(8,128)(2,1)S(1)}, bf16[3,64,64]{2,1,0:T(8,128)(2,1)}, u32[]{:S(2)}) copy-start(bf16[3,64,64]{2,1,0:T(8,128)(2,1)} %get-tuple-element.236) | copy-start | bytes 73732
  45.5 22.8 %copy-start.47 = (bf16[3,64,64]{2,1,0:T(8,128)(2,1)S(1)}, bf16[3,64,64]{2,1,0:T(8,128)(2,1)}, u32[]{:S(2)}) copy-start(bf16[3,64,64]{2,1,0:T(8,128)(2,1)} %get-tuple-element.237) | copy-start | bytes 73732
  87.8 3.0 copy-start.24
  89.5 2.7 copy-start.31
  89.5 2.7 copy-start.28
  89.6 2.7 copy-start.22
  89.6 2.8 copy-start.27
  89.6 2.7 copy-start.16
  89.7 2.8 copy-start.26
  89.7 2.8 copy-start.17
  95.2 14.5 %copy-start.83 = (bf16[3,128,64]{1,2,0:T(8,128)(2,1)S(1)}, bf16[3,128,64]{1,2,0:T(8,128)(2,1)}, u32[]{:S(2)}) copy-start(bf16[3,128,64]{1,2,0:T(8,128)(2,1)} %copy.145) | copy-start | bytes 147460
  95.2 14.7 %copy-start.39 = (bf16[3,128,64]{1,2,0:T(8,128)(2,1)S(1)}, bf16[3,128,64]{1,2,0:T(8,128)(2,1)}, u32[]{:S(2)}) copy-start(bf16[3,128,64]{1,2,0:T(8,128)(2,1)} %copy.146) | copy-start | bytes 147460
  95.2 15.0 %copy-start.38 = (bf16[3,128,64]{1,2,0:T(8,128)(2,1)S(1)}, bf16[3,128,64]{1,2,0:T(8,128)(2,1)}, u32[]{:S(2)}) copy-start(bf16[3,128,64]{1,2,0:T(8,128)(2,1)} %copy.147) | copy-start | bytes 147460
  96.2 14.2 %copy-start.37 = (bf16[3,128,64]{1,2,0:T(8,128)(2,1)S(1)}, bf16[3,128,64]{1,2,0:T(8,128)(2,1)}, u32[]{:S(2)}) copy-start(bf16[3,128,64]{1,2,0:T(8,128)(2,1)} %copy.148) | copy-start | bytes 147460
  96.2 14.4 %copy-start.36 = (bf16[3,128,64]{1,2,0:T(8,128)(2,1)S(1)}, bf16[3,128,64]{1,2,0:T(8,128)(2,1)}, u32[]{:S(2)}) copy-start(bf16[3,128,64]{1,2,0:T(8,128)(2,1)} %copy.149) | copy-start | bytes 147460
  96.2 14.6 %copy-start.35 = (bf16[3,128,64]{1,2,0:T(8,128)(2,1)S(1)}, bf16[3,128,64]{1,2,0:T(8,128)(2,1)}, u32[]{:S(2)}) copy-start(bf16[3,128,64]{1,2,0:T(8,128)(2,1)} %copy.150) | copy-start | bytes 147460
  96.2 14.8 %copy-start.34 = (bf16[3,128,64]{1,2,0:T(8,128)(2,1)S(1)}, bf16[3,128,64]{1,2,0:T(8,128)(2,1)}, u32[]{:S(2)}) copy-start(bf16[3,128,64]{1,2,0:T(8,128)(2,1)} %copy.151) | copy-start | bytes 147460
  96.5 14.8 %copy-start.82 = (bf16[3,128,64]{1,2,0:T(8,128)(2,1)S(1)}, bf16[3,128,64]{1,2,0:T(8,128)(2,1)}, u32[]{:S(2)}) copy-start(bf16[3,128,64]{1,2,0:T(8,128)(2,1)} %copy.153) | copy-start | bytes 147460
  96.6 5.2 %collective-permute-start.5 = (bf16[64,1,1,128]{3,0,2,1:T(8,128)(2,1)S(1)}, bf16[64,1,1,128]{3,0,2,1:T(8,128)(2,1)S(1)}, u32[]{:S(2)}, u32[]{:S(2)}) collective-permute-start(bf16[64,1,1,128]{3,0,2,1:T(8,128)(2,1)S(1)} %fusion.245), channel_id=1, source_target_pairs={{2,0},{4,2},{6,4},{8,6},{10,8},{12,10},{14,12},{16,14},{18,16},{20... | collective-permute-start | bytes 49160 | tf_op jit(solution)/shard_map/ppermute | solution.py:17
  97.9 3.9 collective-permute-start.4
  101.8 6.1 %collective-permute-start.7 = (bf16[64,3,1,128]{3,0,2,1:T(8,128)(2,1)S(1)}, bf16[64,3,1,128]{3,0,2,1:T(8,128)(2,1)S(1)}, u32[]{:S(2)}, u32[]{:S(2)}) collective-permute-start(bf16[64,3,1,128]{3,0,2,1:T(8,128)(2,1)S(1)} %pad_maximum_fusion.18), channel_id=1, source_target_pairs={{1,0},{3,2},{5,4},{7,6},{9,8},{11,10},{13,12},{15,14},{17,16},{19,... | collective-permute-start | bytes 147464 | tf_op jit(solution)/shard_map/ppermute | solution.py:17
  103.1 6.3 %collective-permute-start.6 = (bf16[64,3,1,128]{3,0,2,1:T(8,128)(2,1)S(1)}, bf16[64,3,1,128]{3,0,2,1:T(8,128)(2,1)S(1)}, u32[]{:S(2)}, u32[]{:S(2)}) collective-permute-start(bf16[64,3,1,128]{3,0,2,1:T(8,128)(2,1)S(1)} %pad_maximum_fusion.18), channel_id=1, source_target_pairs={{0,1},{2,3},{4,5},{6,7},{8,9},{10,11},{12,13},{14,15},{16,17},{18,... | collective-permute-start | bytes 147464 | tf_op jit(solution)/shard_map/ppermute | solution.py:15
  109.7 10.5 %copy-start.67 = (bf16[64,128]{1,0:T(8,128)(2,1)}, bf16[64,128]{1,0:T(8,128)(2,1)S(1)}, u32[]{:S(2)}) copy-start(bf16[64,128]{1,0:T(8,128)(2,1)S(1)} %get-tuple-element.238) | copy-start | bytes 49156
  109.7 10.5 %copy-start.69 = (bf16[64,128]{1,0:T(8,128)(2,1)}, bf16[64,128]{1,0:T(8,128)(2,1)S(1)}, u32[]{:S(2)}) copy-start(bf16[64,128]{1,0:T(8,128)(2,1)S(1)} %get-tuple-element.255) | copy-start | bytes 49156
  110.2 9.0 %copy-start.71 = (bf16[64,128]{1,0:T(8,128)(2,1)}, bf16[64,128]{1,0:T(8,128)(2,1)S(1)}, u32[]{:S(2)}) copy-start(bf16[64,128]{1,0:T(8,128)(2,1)S(1)} %get-tuple-element.278) | copy-start | bytes 49156
  111.6 24.4 %collective-permute-start.9 = (bf16[128,1,1,128]{0,3,2,1:T(8,128)(2,1)S(1)}, bf16[128,1,1,128]{0,3,2,1:T(8,128)(2,1)S(1)}, u32[]{:S(2)}, u32[]{:S(2)}) collective-permute-start(bf16[128,1,1,128]{0,3,2,1:T(8,128)(2,1)S(1)} %bitcast.408), channel_id=1, source_target_pairs={{2,0},{4,2},{6,4},{8,6},{10,8},{12,10},{14,12},{16,14},{18,16},{20... | collective-permute-start | bytes 98312 | tf_op jit(solution)/shard_map/ppermute | solution.py:17
  112.9 23.1 %collective-permute-start.8 = (bf16[128,1,1,128]{0,3,2,1:T(8,128)(2,1)S(1)}, bf16[128,1,1,128]{0,3,2,1:T(8,128)(2,1)}, u32[]{:S(2)}, u32[]{:S(2)}) collective-permute-start(bf16[128,1,1,128]{0,3,2,1:T(8,128)(2,1)S(1)} %bitcast.409), channel_id=1, source_target_pairs={{0,2},{2,4},{4,6},{6,8},{8,10},{10,12},{12,14},{14,16},{16,18},{18... | collective-permute-start | bytes 98312 | tf_op jit(solution)/shard_map/ppermute | solution.py:15
  122.4 48.9 %all-to-all-start = ((bf16[2,2,4096]{2,1,0:T(2,128)(2,1)}), bf16[2,2,4096]{2,1,0:T(2,128)(2,1)}, u32[]{:S(2)}, u32[]{:S(2)}) async-start(bf16[2,2,4096]{2,1,0:T(2,128)(2,1)} %reshape.942), calls=%async_computation | async-start | bytes 65536 | tf_op jit(solution)/shard_map/all_to_all | solution.py:129
  126.3 84.4 %all-reduce.8.cloned.1.call-start = ((), (), s32[]{:S(2)}) async-start(), calls=%async_computation.2 | async-start | bytes 1769472 | tf_op jit(solution)/shard_map/psum | solution.py:156
  131.3 12.5 %copy-start.68 = (bf16[64,128]{1,0:T(8,128)(2,1)S(1)}, bf16[64,128]{1,0:T(8,128)(2,1)}, u32[]{:S(2)}) copy-start(bf16[64,128]{1,0:T(8,128)(2,1)} %copy-done.67) | copy-start | bytes 49156
  131.3 12.5 %copy-start.70 = (bf16[64,128]{1,0:T(8,128)(2,1)S(1)}, bf16[64,128]{1,0:T(8,128)(2,1)}, u32[]{:S(2)}) copy-start(bf16[64,128]{1,0:T(8,128)(2,1)} %copy-done.69) | copy-start | bytes 49156
  131.3 12.5 %copy-start.72 = (bf16[64,128]{1,0:T(8,128)(2,1)S(1)}, bf16[64,128]{1,0:T(8,128)(2,1)}, u32[]{:S(2)}) copy-start(bf16[64,128]{1,0:T(8,128)(2,1)} %copy-done.71) | copy-start | bytes 49156
  138.0 6.9 %collective-permute-start.11 = (bf16[128,3,1,128]{0,3,2,1:T(8,128)(2,1)S(1)}, bf16[128,3,1,128]{0,3,2,1:T(8,128)(2,1)S(1)}, u32[]{:S(2)}, u32[]{:S(2)}) collective-permute-start(bf16[128,3,1,128]{0,3,2,1:T(8,128)(2,1)S(1)} %pad_maximum_fusion.17), channel_id=1, source_target_pairs={{1,0},{3,2},{5,4},{7,6},{9,8},{11,10},{13,12},{15,14},{17,16},{19,... | collective-permute-start | bytes 294920 | tf_op jit(solution)/shard_map/ppermute | solution.py:17
  139.3 6.8 %collective-permute-start.10 = (bf16[128,3,1,128]{0,3,2,1:T(8,128)(2,1)S(1)}, bf16[128,3,1,128]{0,3,2,1:T(8,128)(2,1)S(1)}, u32[]{:S(2)}, u32[]{:S(2)}) collective-permute-start(bf16[128,3,1,128]{0,3,2,1:T(8,128)(2,1)S(1)} %pad_maximum_fusion.17), channel_id=1, source_target_pairs={{0,1},{2,3},{4,5},{6,7},{8,9},{10,11},{12,13},{14,15},{16,17},{18,... | collective-permute-start | bytes 294920 | tf_op jit(solution)/shard_map/ppermute | solution.py:15
  157.7 6.4 %collective-permute-start.13 = (bf16[64,1,2,256]{3,2,1,0:T(2,128)(2,1)S(1)}, bf16[64,1,2,256]{3,2,1,0:T(2,128)(2,1)S(1)}, u32[]{:S(2)}, u32[]{:S(2)}) collective-permute-start(bf16[64,1,2,256]{3,2,1,0:T(2,128)(2,1)S(1)} %get-tuple-element.269), channel_id=1, source_target_pairs={{2,0},{4,2},{6,4},{8,6},{10,8},{12,10},{14,12},{16,14},{18,16},{20... | collective-permute-start | bytes 196616 | tf_op jit(solution)/shard_map/ppermute | solution.py:17
  159.0 5.1 %collective-permute-start.12 = (bf16[64,1,2,256]{3,2,1,0:T(2,128)(2,1)S(1)}, bf16[64,1,2,256]{3,2,1,0:T(2,128)(2,1)S(1)}, u32[]{:S(2)}, u32[]{:S(2)}) collective-permute-start(bf16[64,1,2,256]{3,2,1,0:T(2,128)(2,1)S(1)} %get-tuple-element.270), channel_id=1, source_target_pairs={{0,2},{2,4},{4,6},{6,8},{8,10},{10,12},{12,14},{14,16},{16,18},{18... | collective-permute-start | bytes 196616 | tf_op jit(solution)/shard_map/ppermute | solution.py:15
  163.0 7.3 %copy-start.13 = (f32[128,3,64]{2,0,1:T(8,128)S(1)}, f32[128,3,64]{2,0,1:T(8,128)}, u32[]{:S(2)}) copy-start(f32[128,3,64]{2,0,1:T(8,128)} %copy.131) | copy-start | bytes 294916
  164.0 184.8 %all-reduce.12.cloned.1.call-start = ((), (), s32[]{:S(2)}) async-start(), calls=%async_computation.4 | async-start | bytes 3538944 | tf_op jit(solution)/shard_map/psum | solution.py:134
  164.9 9.6 %collective-permute-start.14 = (bf16[64,4,1,256]{3,2,1,0:T(2,128)(2,1)S(1)}, bf16[64,4,1,256]{3,2,1,0:T(2,128)(2,1)S(1)}, u32[]{:S(2)}, u32[]{:S(2)}) collective-permute-start(bf16[64,4,1,256]{3,2,1,0:T(2,128)(2,1)S(1)} %get-tuple-element.259), channel_id=1, source_target_pairs={{0,1},{2,3},{4,5},{6,7},{8,9},{10,11},{12,13},{14,15},{16,17},{18,... | collective-permute-start | bytes 393224 | tf_op jit(solution)/shard_map/ppermute | solution.py:15
  169.0 12.7 %collective-permute-start.15 = (bf16[64,4,1,256]{3,2,1,0:T(2,128)(2,1)S(1)}, bf16[64,4,1,256]{3,2,1,0:T(2,128)(2,1)S(1)}, u32[]{:S(2)}, u32[]{:S(2)}) collective-permute-start(bf16[64,4,1,256]{3,2,1,0:T(2,128)(2,1)S(1)} %get-tuple-element.260), channel_id=1, source_target_pairs={{1,0},{3,2},{5,4},{7,6},{9,8},{11,10},{13,12},{15,14},{17,16},{19,... | collective-permute-start | bytes 393224 | tf_op jit(solution)/shard_map/ppermute | solution.py:17
  171.0 274.5 %all-reduce.10.cloned.1.call-start = ((), (), s32[]{:S(2)}) async-start(), calls=%async_computation.3 | async-start | bytes 1769472 | tf_op jit(solution)/shard_map/psum | solution.py:155
  195.1 15.6 %copy-start.73 = (bf16[3,64,64]{2,1,0:T(8,128)(2,1)S(1)}, bf16[3,64,64]{2,1,0:T(8,128)(2,1)}, u32[]{:S(2)}) copy-start(bf16[3,64,64]{2,1,0:T(8,128)(2,1)} %rev.98) | copy-start | bytes 73732
  (44 other events, 66.6 us)
Sparse Core Ops, SparseCore 0:
  164.1 46.4 all-reduce.7
  216.0 132.7 all-reduce.11
  352.3 93.2 all-reduce.9
